TPU v7x, 32 devices: a whole 2x2x4 slice. The times are simulated.
32 devices in a mesh: rep: 4 (over x, core), fsdp: 8 (over z, y).
Axes of the slice: x: 2, y: 2, z: 4, core: 2. Of those that a mesh axis runs over, the one named last changes fastest.
Arguments:
- tokens: bfloat16 [64, 512, 1024], P('rep', 'fsdp'), may hold values from -6 to 6
- cotangent: bfloat16 [64, 512, 1024], P('rep', 'fsdp'), may hold values from -6 to 6
- lengths: int32 [4, 16], P('rep'), may hold values from 1 to 512, as said below
- deal: int32 [4, 16], P('rep'), may hold values from 0 to 15, each once within a row
- norm_gain: bfloat16 [1024], P('fsdp'), may hold values from 0.099609375 to 1.8984375
- in_weight: bfloat16 [1024, 3072], P('fsdp'), may hold values from -0.1875 to 0.1875
- conv_weight: bfloat16 [1024, 3], P('fsdp'), may hold values from -3 to 3
- out_weight: bfloat16 [1024, 1024], P('fsdp'), may hold values from -0.1875 to 0.1875
- ffn_gain: bfloat16 [1024], P('fsdp'), may hold values from 0.099609375 to 1.8984375
- gate_weight: bfloat16 [1024, 4608], P('fsdp'), may hold values from -0.1875 to 0.1875
- up_weight: bfloat16 [1024, 4608], P('fsdp'), may hold values from -0.1875 to 0.1875
- down_weight: bfloat16 [4608, 1024], P('fsdp'), may hold values from -0.1875 to 0.1875
Outputs:
- block_out: bfloat16 [64, 512, 1024], P('rep', 'fsdp')
- block_grad: bfloat16 [64, 512, 1024], P('rep', 'fsdp')
- norm_gain_grad: float32 [1024], P('fsdp')
- in_grad: float32 [1024, 3072], P('fsdp')
- conv_grad: float32 [1024, 3], P('fsdp')
- out_grad: float32 [1024, 1024], P('fsdp')
- ffn_gain_grad: float32 [1024], P('fsdp')
- gate_grad: float32 [1024, 4608], P('fsdp')
- up_grad: float32 [1024, 4608], P('fsdp')
- down_grad: float32 [4608, 1024], P('fsdp')
Inputs may be any that keep to these rules, and one draw needn't show every extreme that they name: In each row, the 2 lengths of slots 2 i to 2 i + 1 sum to at most 768; in each row one such set sums to exactly 768 and holds a length of exactly 512. `deal`: each row is a permutation of the group's sequence numbers.
All inputs are finite; a program needn't handle non-finite values.
Results may differ from a plain program's by a relative error of at most 0.018.
Values may be sent and summed in bfloat16 or wider, within the bound.
A program may use at most 256 MiB of HBM per device.

v0:
```python
import jax
import jax.numpy as jnp
from jax import lax
from jax.sharding import PartitionSpec as P

SLOT = 512
CAP_DEV = 768
EPS = 1e-05


def row_scale(values):
    return lax.rsqrt(jnp.mean(values * values, axis=-1, keepdims=True) + EPS)


def norm_back(grad_unit, unit_rows, scale_rows):
    return scale_rows * (
        grad_unit - unit_rows * jnp.mean(grad_unit * unit_rows, axis=-1, keepdims=True)
    )


def lag_rows(values, amount):
    return jnp.pad(values, ((amount, 0), (0, 0)))[: values.shape[0]]


def lead_rows(values, amount):
    return jnp.pad(values, ((0, amount), (0, 0)))[amount:]


def over_rows(left_side, right_side):
    return lax.dot_general(
        left_side, right_side, (((0,), (0,)), ((), ())), preferred_element_type=jnp.float32
    )


def over_cols(left_side, right_side):
    return lax.dot_general(
        left_side, right_side, (((1,), (1,)), ((), ())), preferred_element_type=jnp.float32
    )


def pack_tables(lengths):
    group_len = lengths[0]
    seq_dev = group_len.shape[0] // lax.axis_size("fsdp")
    own_len = lax.dynamic_slice_in_dim(group_len, lax.axis_index("fsdp") * seq_dev, seq_dev)
    seq_ends = jnp.cumsum(own_len)
    starts = seq_ends - own_len
    total_len = seq_ends[seq_dev - 1]
    slot_ids = jnp.arange(seq_dev, dtype=jnp.int32)
    row_ids = jnp.arange(CAP_DEV, dtype=jnp.int32)
    which_seq = jnp.minimum(
        jnp.sum((row_ids[:, None] >= seq_ends[None, :]).astype(jnp.int32), axis=1), seq_dev - 1
    )
    row_start = jnp.sum(
        jnp.where(which_seq[:, None] == slot_ids[None, :], starts[None, :], 0), axis=1
    )
    row_live = row_ids < total_len
    position = jnp.where(row_live, row_ids - row_start, 0)
    source = jnp.where(row_live, which_seq * SLOT + position, 0)
    lag_masks = (
        (position >= 1).astype(jnp.float32)[:, None],
        (position >= 2).astype(jnp.float32)[:, None],
    )
    cell_ids = jnp.arange(seq_dev * SLOT, dtype=jnp.int32)
    cell_pick = (cell_ids // SLOT)[:, None] == slot_ids[None, :]
    cell_pos = cell_ids % SLOT
    cell_len = jnp.sum(jnp.where(cell_pick, own_len[None, :], 0), axis=1)
    cell_start = jnp.sum(jnp.where(cell_pick, starts[None, :], 0), axis=1)
    cell_live = cell_pos < cell_len
    back_index = jnp.where(cell_live, cell_start + cell_pos, 0)
    return (source, row_live, lag_masks, back_index, cell_live)


def to_rows(slot_values, source):
    width = slot_values.shape[2]
    return jnp.take(slot_values.reshape(-1, width), source, axis=0).astype(jnp.float32)


def to_slots(packed_rows, back_index, cell_live, seq_dev):
    cells = jnp.where(cell_live[:, None], jnp.take(packed_rows, back_index, axis=0), 0.0)
    return cells.astype(jnp.bfloat16).reshape(seq_dev, SLOT, packed_rows.shape[1])


def to_sources(received, deal_row):
    slot_ids = jnp.arange(deal_row.shape[0], dtype=jnp.int32)
    inverse = jnp.sum(
        jnp.where(deal_row[None, :] == slot_ids[:, None], slot_ids[None, :], 0), axis=1
    )
    return jnp.take(received, inverse, axis=0)


def forward_pass(token_rows, mix_set, ffn_set, lag_masks):
    norm_gain, in_weight, conv_weight, out_weight = mix_set
    ffn_gain, gate_weight, up_weight, down_weight = ffn_set
    width = in_weight.shape[0]
    scale_one = row_scale(token_rows)
    unit_one = token_rows * scale_one
    normed_one = (unit_one * norm_gain.astype(jnp.float32)).astype(jnp.bfloat16)
    projected = jnp.dot(normed_one, in_weight, preferred_element_type=jnp.float32)
    b_gate = projected[:, :width]
    c_gate = projected[:, width : 2 * width]
    x_value = projected[:, 2 * width :]
    product = b_gate * x_value
    lag_one = lag_rows(product, 1) * lag_masks[0]
    lag_two = lag_rows(product, 2) * lag_masks[1]
    taps = conv_weight.astype(jnp.float32)
    convolved = taps[:, 0] * lag_two + taps[:, 1] * lag_one + taps[:, 2] * product
    gated = (c_gate * convolved).astype(jnp.bfloat16)
    middle = token_rows + jnp.dot(gated, out_weight, preferred_element_type=jnp.float32)
    scale_two = row_scale(middle)
    unit_two = middle * scale_two
    normed_two = (unit_two * ffn_gain.astype(jnp.float32)).astype(jnp.bfloat16)
    gate_lin = jnp.dot(normed_two, gate_weight, preferred_element_type=jnp.float32)
    up_lin = jnp.dot(normed_two, up_weight, preferred_element_type=jnp.float32)
    hidden = (jax.nn.silu(gate_lin) * up_lin).astype(jnp.bfloat16)
    output = middle + jnp.dot(hidden, down_weight, preferred_element_type=jnp.float32)
    return (
        scale_one,
        unit_one,
        normed_one,
        b_gate,
        c_gate,
        x_value,
        product,
        lag_one,
        lag_two,
        convolved,
        gated,
        scale_two,
        unit_two,
        normed_two,
        gate_lin,
        up_lin,
        hidden,
        output,
    )


def backward_pass(saved, mix_set, ffn_set, lag_masks, grad_out):
    (
        scale_one,
        unit_one,
        normed_one,
        b_gate,
        c_gate,
        x_value,
        product,
        lag_one,
        lag_two,
        convolved,
        gated,
        scale_two,
        unit_two,
        normed_two,
        gate_lin,
        up_lin,
        hidden,
        output,
    ) = saved
    norm_gain, in_weight, conv_weight, out_weight = mix_set
    ffn_gain, gate_weight, up_weight, down_weight = ffn_set
    grad_ffn = grad_out.astype(jnp.bfloat16)
    down_grad = over_rows(hidden, grad_ffn)
    grad_hidden = over_cols(grad_ffn, down_weight)
    sigma = jax.nn.sigmoid(gate_lin)
    grad_gate = (grad_hidden * up_lin * sigma * (1.0 + gate_lin * (1.0 - sigma))).astype(
        jnp.bfloat16
    )
    grad_up = (grad_hidden * gate_lin * sigma).astype(jnp.bfloat16)
    gate_grad = over_rows(normed_two, grad_gate)
    up_grad = over_rows(normed_two, grad_up)
    grad_normed_two = over_cols(grad_gate, gate_weight) + over_cols(grad_up, up_weight)
    ffn_gain_grad = jnp.sum(grad_normed_two * unit_two, axis=0)
    grad_middle = grad_out + norm_back(
        grad_normed_two * ffn_gain.astype(jnp.float32), unit_two, scale_two
    )
    grad_mixed = grad_middle.astype(jnp.bfloat16)
    out_grad = over_rows(gated, grad_mixed)
    grad_gated = over_cols(grad_mixed, out_weight)
    grad_c = grad_gated * convolved
    grad_conv = grad_gated * c_gate
    conv_grad = jnp.stack(
        [
            jnp.sum(grad_conv * lag_two, axis=0),
            jnp.sum(grad_conv * lag_one, axis=0),
            jnp.sum(grad_conv * product, axis=0),
        ],
        axis=1,
    )
    taps = conv_weight.astype(jnp.float32)
    grad_product = (
        taps[:, 2] * grad_conv
        + taps[:, 1] * lead_rows(grad_conv * lag_masks[0], 1)
        + taps[:, 0] * lead_rows(grad_conv * lag_masks[1], 2)
    )
    grad_projected = jnp.concatenate(
        [grad_product * x_value, grad_c, grad_product * b_gate], axis=1
    ).astype(jnp.bfloat16)
    in_grad = over_rows(normed_one, grad_projected)
    grad_normed_one = over_cols(grad_projected, in_weight)
    norm_gain_grad = jnp.sum(grad_normed_one * unit_one, axis=0)
    grad_tokens = grad_middle + norm_back(
        grad_normed_one * norm_gain.astype(jnp.float32), unit_one, scale_one
    )
    return (
        grad_tokens,
        (
            norm_gain_grad,
            in_grad,
            conv_grad,
            out_grad,
            ffn_gain_grad,
            gate_grad,
            up_grad,
            down_grad,
        ),
    )


def body(
    tokens,
    cotangent,
    lengths,
    deal,
    norm_gain,
    in_weight,
    conv_weight,
    out_weight,
    ffn_gain,
    gate_weight,
    up_weight,
    down_weight,
):
    source, row_live, lag_masks, back_index, cell_live = pack_tables(lengths)
    seq_dev = deal.shape[1] // lax.axis_size("fsdp")
    deal_row = deal[0]
    sent_tokens = jnp.take(tokens, deal_row, axis=0)
    sent_cot = jnp.take(cotangent, deal_row, axis=0)
    slot_tokens, slot_cot = (
        lax.all_to_all(sent_tokens, "fsdp", split_axis=0, concat_axis=1, tiled=True),
        lax.all_to_all(sent_cot, "fsdp", split_axis=0, concat_axis=1, tiled=True),
    )
    token_rows = to_rows(slot_tokens, source)
    cot_rows = jnp.where(row_live[:, None], to_rows(slot_cot, source), 0.0)
    mix_set = (
        lax.all_gather(norm_gain, "fsdp", axis=0, tiled=True),
        lax.all_gather(in_weight, "fsdp", axis=0, tiled=True),
        lax.all_gather(conv_weight, "fsdp", axis=0, tiled=True),
        lax.all_gather(out_weight, "fsdp", axis=0, tiled=True),
    )
    ffn_set = (
        lax.all_gather(ffn_gain, "fsdp", axis=0, tiled=True),
        lax.all_gather(gate_weight, "fsdp", axis=0, tiled=True),
        lax.all_gather(up_weight, "fsdp", axis=0, tiled=True),
        lax.all_gather(down_weight, "fsdp", axis=0, tiled=True),
    )
    saved = forward_pass(token_rows, mix_set, ffn_set, lag_masks)
    out_slots = to_slots(saved[-1], back_index, cell_live, seq_dev)
    out_back = lax.all_to_all(out_slots, "fsdp", split_axis=1, concat_axis=0, tiled=True)
    block_out = to_sources(out_back, deal_row)
    again_slots = lax.all_to_all(sent_tokens, "fsdp", split_axis=0, concat_axis=1, tiled=True)
    again_rows = to_rows(again_slots, source)
    mix_back = (
        lax.all_gather(norm_gain, "fsdp", axis=0, tiled=True),
        lax.all_gather(in_weight, "fsdp", axis=0, tiled=True),
        lax.all_gather(conv_weight, "fsdp", axis=0, tiled=True),
        lax.all_gather(out_weight, "fsdp", axis=0, tiled=True),
    )
    ffn_back = (
        lax.all_gather(ffn_gain, "fsdp", axis=0, tiled=True),
        lax.all_gather(gate_weight, "fsdp", axis=0, tiled=True),
        lax.all_gather(up_weight, "fsdp", axis=0, tiled=True),
        lax.all_gather(down_weight, "fsdp", axis=0, tiled=True),
    )
    saved_back = forward_pass(again_rows, mix_back, ffn_back, lag_masks)
    grad_rows, weight_grads = backward_pass(saved_back, mix_back, ffn_back, lag_masks, cot_rows)
    grad_slots = to_slots(grad_rows, back_index, cell_live, seq_dev)
    grad_back = lax.all_to_all(grad_slots, "fsdp", split_axis=1, concat_axis=0, tiled=True)
    block_grad = to_sources(grad_back, deal_row)
    shares = (
        lax.psum_scatter(
            weight_grads[0].astype(jnp.bfloat16), "fsdp", scatter_dimension=0, tiled=True
        ).astype(jnp.float32),
        lax.psum_scatter(
            weight_grads[1].astype(jnp.bfloat16), "fsdp", scatter_dimension=0, tiled=True
        ).astype(jnp.float32),
        lax.psum_scatter(
            weight_grads[2].astype(jnp.bfloat16), "fsdp", scatter_dimension=0, tiled=True
        ).astype(jnp.float32),
        lax.psum_scatter(
            weight_grads[3].astype(jnp.bfloat16), "fsdp", scatter_dimension=0, tiled=True
        ).astype(jnp.float32),
        lax.psum_scatter(
            weight_grads[4].astype(jnp.bfloat16), "fsdp", scatter_dimension=0, tiled=True
        ).astype(jnp.float32),
        lax.psum_scatter(
            weight_grads[5].astype(jnp.bfloat16), "fsdp", scatter_dimension=0, tiled=True
        ).astype(jnp.float32),
        lax.psum_scatter(
            weight_grads[6].astype(jnp.bfloat16), "fsdp", scatter_dimension=0, tiled=True
        ).astype(jnp.float32),
        lax.psum_scatter(
            weight_grads[7].astype(jnp.bfloat16), "fsdp", scatter_dimension=0, tiled=True
        ).astype(jnp.float32),
    )
    summed = (
        lax.psum(shares[0].astype(jnp.bfloat16), "rep").astype(jnp.float32),
        lax.psum(shares[1].astype(jnp.bfloat16), "rep").astype(jnp.float32),
        lax.psum(shares[2].astype(jnp.bfloat16), "rep").astype(jnp.float32),
        lax.psum(shares[3].astype(jnp.bfloat16), "rep").astype(jnp.float32),
        lax.psum(shares[4].astype(jnp.bfloat16), "rep").astype(jnp.float32),
        lax.psum(shares[5].astype(jnp.bfloat16), "rep").astype(jnp.float32),
        lax.psum(shares[6].astype(jnp.bfloat16), "rep").astype(jnp.float32),
        lax.psum(shares[7].astype(jnp.bfloat16), "rep").astype(jnp.float32),
    )
    return (
        block_out,
        block_grad,
        summed[0],
        summed[1],
        summed[2],
        summed[3],
        summed[4],
        summed[5],
        summed[6],
        summed[7],
    )


def solution(mesh):
    placed = (
        P("rep", "fsdp", None),
        P("rep", "fsdp", None),
        P("rep", None),
        P("rep", None),
        P("fsdp"),
        P("fsdp", None),
        P("fsdp", None),
        P("fsdp", None),
        P("fsdp"),
        P("fsdp", None),
        P("fsdp", None),
        P("fsdp", None),
    )
    return jax.shard_map(
        body,
        mesh=mesh,
        in_specs=placed,
        out_specs=(
            P("rep", "fsdp", None),
            P("rep", "fsdp", None),
            P("fsdp"),
            P("fsdp", None),
            P("fsdp", None),
            P("fsdp", None),
            P("fsdp"),
            P("fsdp", None),
            P("fsdp", None),
            P("fsdp", None),
        ),
        check_vma=False,
    )
```

profile of v0, /device:TPU:0, one launch (start us, length us, event | category | flops | bytes accessed | tf_op | source)
XLA Modules:
  0.0 1630.6 jit_solution(14455915364186069048)
XLA Ops:
  19.7 92.7 %all_to_all.71 = bf16[16,64,1024]{2,1,0:T(8,128)(2,1)} all-to-all(bf16[16,64,1024]{2,1,0:T(8,128)(2,1)S(1)} %get-tuple-element.59), channel_id=1, replica_groups=mesh['rep'=4,'fsdp'=8] {'fsdp'}, dimensions={0} | all-to-all | bytes 4194304 | tf_op jit(solution)/shard_map/all_to_all | solution.py:239
  119.0 68.1 %all-gather = bf16[8,1,128]{2,1,0:T(2,128)(2,1)S(1)} all-gather(bf16[1,1,128]{2,1,0:T(2,128)(2,1)S(1)} %bitcast.88), channel_id=1, replica_groups=mesh['rep'=4,'fsdp'=8] {'fsdp'}, dimensions={0}, use_global_device_ids=true | all-gather | bytes 2304 | tf_op jit(solution)/shard_map/all_gather | solution.py:245
  187.1 30.4 %all-gather.1 = bf16[8,1,128]{2,1,0:T(2,128)(2,1)S(1)} all-gather(bf16[1,1,128]{2,1,0:T(2,128)(2,1)S(1)} %bitcast.89), channel_id=1, replica_groups=mesh['rep'=4,'fsdp'=8] {'fsdp'}, dimensions={0}, use_global_device_ids=true | all-gather | bytes 2304 | tf_op jit(solution)/shard_map/all_gather | solution.py:251
  217.5 16.5 %all_gather.34 = bf16[1024,3]{0,1:T(4,128)(2,1)S(1)} all-gather(bf16[128,3]{0,1:T(4,128)(2,1)S(1)} %copy-done.28), channel_id=1, replica_groups=mesh['rep'=4,'fsdp'=8] {'fsdp'}, dimensions={0}, use_global_device_ids=true | all-gather | bytes 6912 | tf_op jit(solution)/shard_map/all_gather | solution.py:247
  273.8 100.0 %all-gather.12.cloned.1.call-done = bf16[1024,4608]{1,0:T(8,128)(2,1)} async-done(((bf16[128,4608]{1,0:T(8,128)(2,1)}), bf16[1024,4608]{1,0:T(8,128)(2,1)}) %all-gather.12.cloned.1.call-update) | async-done | bytes 9437200 | tf_op jit(solution)/shard_map/all_gather | solution.py:252
  373.8 13.4 fusion.46
  387.1 125.0 %all-gather.14.cloned.1.call-done = bf16[1024,4608]{1,0:T(8,128)(2,1)} async-done(((bf16[128,4608]{1,0:T(8,128)(2,1)}), bf16[1024,4608]{1,0:T(8,128)(2,1)}) %all-gather.14.cloned.1.call-update) | async-done | bytes 9437200 | tf_op jit(solution)/shard_map/all_gather | solution.py:253
  512.1 13.7 fusion.47
  525.7 124.7 %all-gather.16.cloned.1.call-done = bf16[4608,1024]{1,0:T(8,128)(2,1)} async-done(((bf16[576,1024]{1,0:T(8,128)(2,1)}), bf16[4608,1024]{1,0:T(8,128)(2,1)}) %all-gather.16.cloned.1.call-update) | async-done | bytes 9437200 | tf_op jit(solution)/shard_map/all_gather | solution.py:254
  650.4 28.2 %multiply_convert_fusion = (bf16[768,4608]{1,0:T(8,128)(2,1)}, bf16[768,4608]{1,0:T(8,128)(2,1)}, bf16[768,4608]{1,0:T(8,128)(2,1)}) fusion(f32[768,4608]{1,0:T(8,128)} %fusion.46, f32[768,4608]{1,0:T(8,128)} %fusion.47, bf16[4608,1024]{1,0:T(8,128)(2,1)} %all-gather.16.cloned.1.call-done, pred[768]{0:T(1024)(128)(4,1)S(1)} %iota_compare_fusion.2, ...), kind=kOutput, calls=%fused_computation.8 | convolution fusion | flops 7307526144 | bytes 60556800 | tf_op jit(solution)/shard_map/dot_general | solution.py:36
  678.6 13.5 fusion.48
  692.1 11.2 multiply_reduce_fusion
  738.2 13.2 convolution_convert_fusion.2
  751.5 12.9 convolution_convert_fusion.1
  765.9 13.5 convolution_convert_fusion
  780.1 12.6 convolution_add_fusion.1
  829.5 54.8 %all-to-all-done.1 = bf16[2,512,1024]{2,0,1:T(2,128)(2,1)} async-done(((bf16[2,512,1024]{2,0,1:T(2,128)(2,1)}), bf16[2,512,1024]{2,0,1:T(2,128)(2,1)}, u32[]{:S(2)}, u32[]{:S(2)}) %all-to-all-start.1) | async-done | bytes 2097184 | tf_op jit(solution)/shard_map/all_to_all | solution.py:258
  889.1 70.7 %reduce-scatter.9.cloned.1.call-done = bf16[128,3072]{1,0:T(8,128)(2,1)} async-done(((bf16[1024,3072]{1,0:T(8,128)(2,1)}), bf16[128,3072]{1,0:T(8,128)(2,1)}) %reduce-scatter.9.cloned.1.call-update) | async-done | bytes 786448 | tf_op jit(solution)/shard_map/reduce_scatter | solution.py:283
  959.8 164.2 %reduce-scatter.13.cloned.1.call-done = bf16[128,4608]{1,0:T(8,128)(2,1)} async-done(((bf16[1024,4608]{1,0:T(8,128)(2,1)}), bf16[128,4608]{1,0:T(8,128)(2,1)}) %reduce-scatter.13.cloned.1.call-update) | async-done | bytes 1179664 | tf_op jit(solution)/shard_map/reduce_scatter | solution.py:295
  1124.0 166.2 %reduce-scatter.15.cloned.1.call-done = bf16[128,4608]{1,0:T(8,128)(2,1)} async-done(((bf16[1024,4608]{1,0:T(8,128)(2,1)}), bf16[128,4608]{1,0:T(8,128)(2,1)}) %reduce-scatter.15.cloned.1.call-update) | async-done | bytes 1179664 | tf_op jit(solution)/shard_map/reduce_scatter | solution.py:298
  1290.2 166.0 %reduce-scatter.17.cloned.1.call-done = bf16[576,1024]{1,0:T(8,128)(2,1)} async-done(((bf16[4608,1024]{1,0:T(8,128)(2,1)}), bf16[576,1024]{1,0:T(8,128)(2,1)}) %reduce-scatter.17.cloned.1.call-update) | async-done | bytes 1179664 | tf_op jit(solution)/shard_map/reduce_scatter | solution.py:301
  1457.6 19.5 %all-reduce.6 = (bf16[1024]{0:T(1024)(128)(2,1)S(1)}, bf16[1024]{0:T(1024)(128)(2,1)S(1)}) all-reduce(bf16[1024]{0:T(1024)(128)(2,1)S(1)} %get-tuple-element.18, bf16[1024]{0:T(1024)(128)(2,1)S(1)} %get-tuple-element.13), channel_id=2, replica_groups=mesh['rep'=4,'fsdp'=8] {'fsdp'}, use_global_device_ids=true, to_apply=%region_11.15.clone | all-reduce | flops 2048 | bytes 8192
  1477.2 43.3 %reduce-scatter.19.cloned.1.call-done = bf16[128,3]{1,0:T(8,128)(2,1)} async-done(((bf16[1024,3]{1,0:T(8,128)(2,1)}), bf16[128,3]{1,0:T(8,128)(2,1)}) %reduce-scatter.19.cloned.1.call-update) | async-done | bytes 784
  1545.1 69.7 %all-reduce.11.cloned.1.call-done = (bf16[128,3072]{1,0:T(8,128)(2,1)}, bf16[128,1024]{1,0:T(8,128)(2,1)}, bf16[128,4608]{1,0:T(8,128)(2,1)}, bf16[128,4608]{1,0:T(8,128)(2,1)}, bf16[576,1024]{1,0:T(8,128)(2,1)}) async-done(((bf16[128,3072]{1,0:T(8,128)(2,1)}, bf16[128,1024]{1,0:T(8,128)(2,1)}, bf16[128,4608]{1,0:T(8,128)(2,1)}, bf16[128,4608]{1,0:T(8,128)(2,1)}, bf16[576,1024]{1,0:T(8,128)(2,1)}), ...) | async-done | bytes 4587536 | tf_op jit(solution)/shard_map/psum | solution.py:307
  (182 shorter events, 170.9 us)
Async XLA Ops:
  7.2 244.2 %all-gather.8.cloned.1.call-start = ((), (), s32[]{:S(2)}) async-start(), calls=%async_computation.10 | async-start | bytes 7077888 | tf_op jit(solution)/shard_map/all_gather | solution.py:246
  7.9 258.6 %all-gather.10.cloned.1.call-start = ((), (), s32[]{:S(2)}) async-start(), calls=%async_computation.11 | async-start | bytes 2359296 | tf_op jit(solution)/shard_map/all_gather | solution.py:248
  8.7 365.1 %all-gather.12.cloned.1.call-start = ((), (), s32[]{:S(2)}) async-start(), calls=%async_computation.12 | async-start | bytes 10616832 | tf_op jit(solution)/shard_map/all_gather | solution.py:252
  9.4 502.7 %all-gather.14.cloned.1.call-start = ((), (), s32[]{:S(2)}) async-start(), calls=%async_computation.13 | async-start | bytes 10616832 | tf_op jit(solution)/shard_map/all_gather | solution.py:253
  10.0 640.4 %all-gather.16.cloned.1.call-start = ((), (), s32[]{:S(2)}) async-start(), calls=%async_computation.14 | async-start | bytes 10616832 | tf_op jit(solution)/shard_map/all_gather | solution.py:254
  112.5 74.6 %copy-start.30 = (bf16[128]{0:T(256)(128)(2,1)S(1)}, bf16[128]{0:T(256)(128)(2,1)}, u32[]{:S(2)}) copy-start(bf16[128]{0:T(256)(128)(2,1)} %param.26) | copy-start | bytes 772
  112.5 105.1 %copy-start.28 = (bf16[128,3]{0,1:T(4,128)(2,1)S(1)}, bf16[128,3]{0,1:T(4,128)(2,1)}, u32[]{:S(2)}) copy-start(bf16[128,3]{0,1:T(4,128)(2,1)} %param.24) | copy-start | bytes 2308
  112.5 125.0 %all-to-all-start.2 = ((bf16[16,64,1024]{2,1,0:T(8,128)(2,1)}), bf16[16,64,1024]{2,1,0:T(8,128)(2,1)}, u32[]{:S(2)}, u32[]{:S(2)}) async-start(bf16[16,64,1024]{2,1,0:T(8,128)(2,1)} %get-tuple-element.58), calls=%async_computation.2 | async-start | bytes 4194304 | tf_op jit(solution)/shard_map/all_to_all | solution.py:240
  117.6 771.5 %reduce-scatter.11.cloned.1.call-start = ((), (), s32[]{:S(2)}) async-start(), calls=%async_computation.16 | async-start | bytes 2359296 | tf_op jit(solution)/shard_map/reduce_scatter | solution.py:289
  678.6 13.5 copy-start.9
  678.6 13.5 copy-start.34
  692.1 11.3 copy-start.13
  710.0 249.8 %reduce-scatter.9.cloned.1.call-start = ((), (), s32[]{:S(2)}) async-start(), calls=%async_computation.15 | async-start | bytes 7077888 | tf_op jit(solution)/shard_map/reduce_scatter | solution.py:283
  736.8 387.2 %reduce-scatter.13.cloned.1.call-start = ((), (), s32[]{:S(2)}) async-start(), calls=%async_computation.17 | async-start | bytes 10616832 | tf_op jit(solution)/shard_map/reduce_scatter | solution.py:295
  751.5 538.7 %reduce-scatter.15.cloned.1.call-start = ((), (), s32[]{:S(2)}) async-start(), calls=%async_computation.18 | async-start | bytes 10616832 | tf_op jit(solution)/shard_map/reduce_scatter | solution.py:298
  764.5 691.7 %reduce-scatter.17.cloned.1.call-start = ((), (), s32[]{:S(2)}) async-start(), calls=%async_computation.19 | async-start | bytes 10616832 | tf_op jit(solution)/shard_map/reduce_scatter | solution.py:301
  798.1 10.0 copy-start.4
  798.1 10.0 copy-start.7
  821.7 62.7 %all-to-all-start.1 = ((bf16[2,512,1024]{2,0,1:T(2,128)(2,1)}), bf16[2,512,1024]{2,0,1:T(2,128)(2,1)}, u32[]{:S(2)}, u32[]{:S(2)}) async-start(bf16[2,512,1024]{2,0,1:T(2,128)(2,1)} %copy.39), calls=%async_computation.1 | async-start | bytes 4194304 | tf_op jit(solution)/shard_map/all_to_all | solution.py:258
  884.4 647.9 %all-to-all-start.3 = ((bf16[2,512,1024]{2,0,1:T(2,128)(2,1)}), bf16[2,512,1024]{2,0,1:T(2,128)(2,1)S(1)}, u32[]{:S(2)}, u32[]{:S(2)}) async-start(bf16[2,512,1024]{2,0,1:T(2,128)(2,1)} %copy.43), calls=%async_computation.3 | async-start | bytes 4194304 | tf_op jit(solution)/shard_map/all_to_all | solution.py:277
  888.0 568.2 %copy-start.33 = (u32[32]{0:T(128)S(1)}, u32[32]{0:T(128)}, u32[]{:S(2)}) copy-start(u32[32]{0:T(128)} %constant.108) | copy-start | bytes 388
  888.0 569.4 %copy-start.32 = (s32[1,16]{1,0:T(1,128)S(1)}, s32[1,16]{1,0:T(1,128)}, u32[]{:S(2)}) copy-start(s32[1,16]{1,0:T(1,128)} %param.21) | copy-start | bytes 196
  888.0 632.5 %reduce-scatter.19.cloned.1.call-start = ((), (), s32[]{:S(2)}) async-start(), calls=%async_computation.20 | async-start | bytes 294912
  889.0 725.7 %all-reduce.11.cloned.1.call-start = ((), (), s32[]{:S(2)}) async-start(), calls=%async_computation.21 | async-start | bytes 9175040 | tf_op jit(solution)/shard_map/psum | solution.py:307
  (26 other events, 83.6 us)
Sparse Core Ops, SparseCore 0:
  10.2 174.4 all-gather.7
  186.8 48.0 all-gather.9
  237.1 136.5 all-gather.11
  375.8 136.2 all-gather.13
  514.1 136.2 all-gather.15
  710.1 65.9 reduce-scatter.10
  779.7 180.0 reduce-scatter.8
  963.4 160.5 reduce-scatter.12
  1127.6 162.5 reduce-scatter.14
  1293.6 162.5 reduce-scatter.16
  1460.1 60.3 reduce-scatter.18
  1523.1 91.6 all-reduce.10
where the time goes:
time: 1640 us; the launch traced here: 1630 us
  waiting for transfers between devices  1090 us (66%)
  blocking collectives  233 us (14%)
  matrix products  175 us (11%)
  local copies, waits for them, and re-layouts  66 us (4%)
  other arithmetic  39.3 us (2%)
    reduce_scatter x1, waiting for transfers between devices, body(): lax.psum_scatter(weight_grads[6].astype(jnp.bfloat16), 'fsdp', scatter_di...  166 us
    reduce_scatter x1, waiting for transfers between devices, body(): lax.psum_scatter(weight_grads[7].astype(jnp.bfloat16), 'fsdp', scatter_di...  166 us
    reduce_scatter x1, waiting for transfers between devices, body(): lax.psum_scatter(weight_grads[5].astype(jnp.bfloat16), 'fsdp', scatter_di...  164 us
    all_gather x1, waiting for transfers between devices, body(): lax.all_gather(up_weight, 'fsdp', axis=0, tiled=True)  125 us
    all_gather x1, waiting for transfers between devices, body(): lax.all_gather(down_weight, 'fsdp', axis=0, tiled=True)  125 us
    all_gather x1, waiting for transfers between devices, body(): lax.all_gather(gate_weight, 'fsdp', axis=0, tiled=True)  100 us
    all_to_all x1, blocking collectives, body(): lax.all_to_all(sent_tokens, 'fsdp', split_axis=0, concat_axis=1, tiled=True)  92.7 us
    dot_general x5, matrix products, over_cols(): lax.dot_general(left_side, right_side, (((1,), (1,)), ((), ())), preferre...  73 us
  transfers between devices with their start and end apart: 15, of which 10 were waited for; matrix products, arithmetic and copies ran while one was open for 12% of the time, Pallas kernels for 0%

commit v1 on v0

--- a/solution.py
+++ b/solution.py
@@ -6,6 +6,18 @@
 SLOT = 512
 CAP_DEV = 768
 EPS = 1e-05
+
+
+def doubled_up(shard, axis, dim):
+    ways, here = (lax.axis_size(axis), lax.axis_index(axis))
+    grown, reach = (shard, 1)
+    while reach < ways:
+        theirs = lax.ppermute(grown, axis, [(d, d ^ reach) for d in range(ways)])
+        mine_first = jnp.concatenate([grown, theirs], axis=dim)
+        theirs_first = jnp.concatenate([theirs, grown], axis=dim)
+        grown = jnp.where(here & reach == 0, mine_first, theirs_first)
+        reach = 2 * reach
+    return grown
 
 
 def row_scale(values):
@@ -251,7 +263,7 @@
         lax.all_gather(ffn_gain, "fsdp", axis=0, tiled=True),
         lax.all_gather(gate_weight, "fsdp", axis=0, tiled=True),
         lax.all_gather(up_weight, "fsdp", axis=0, tiled=True),
-        lax.all_gather(down_weight, "fsdp", axis=0, tiled=True),
+        doubled_up(down_weight, "fsdp", 0),
     )
     saved = forward_pass(token_rows, mix_set, ffn_set, lag_masks)
     out_slots = to_slots(saved[-1], back_index, cell_live, seq_dev)

time: 1640 us -> 1840 us (1.12)
  waiting for transfers between devices: 1090 us -> 1270 us
    ppermute x0 -> x3, waiting for transfers between devices: none -> 412 us  [doubled_up(): theirs = lax.ppermute(grown, axis, [(d, d ^ reach) for d in range(ways)])]
    reduce_scatter x1, waiting for transfers between devices: 164 us -> 0.02 us  [body(): lax.psum_scatter(weight_grads[5].astype(jnp.bfloat16), 'fsdp', scatter_di...]
    reduce_scatter x1, waiting for transfers between devices: 70.7 us -> 0.02 us  [body(): lax.psum_scatter(weight_grads[1].astype(jnp.bfloat16), 'fsdp', scatter_di...]
    all_to_all x1, waiting for transfers between devices: 54.8 us -> 95.6 us  [body(): lax.all_to_all(out_slots, 'fsdp', split_axis=1, concat_axis=0, tiled=True)]
    reduce_scatter x1, waiting for transfers between devices: 166 us -> 134 us  [body(): lax.psum_scatter(weight_grads[6].astype(jnp.bfloat16), 'fsdp', scatter_di...]
  transfers between devices with their start and end apart: 15 -> 18, of which waited for: 10 -> 11; matrix products, arithmetic and copies ran while one was open for 12% -> 12% of each run, Pallas kernels for 0% -> 0%
where the time goes in v1:
time: 1840 us; the launch traced here: 1830 us
  waiting for transfers between devices  1270 us (69%)
  blocking collectives  233 us (13%)
  matrix products  177 us (10%)
  local copies, waits for them, and re-layouts  65.3 us (4%)
  other arithmetic  48.5 us (3%)
    ppermute x3, waiting for transfers between devices, doubled_up(): theirs = lax.ppermute(grown, axis, [(d, d ^ reach) for d in range(ways)])  412 us
    reduce_scatter x1, waiting for transfers between devices, body(): lax.psum_scatter(weight_grads[7].astype(jnp.bfloat16), 'fsdp', scatter_di...  166 us
    reduce_scatter x1, waiting for transfers between devices, body(): lax.psum_scatter(weight_grads[6].astype(jnp.bfloat16), 'fsdp', scatter_di...  134 us
    all_gather x1, waiting for transfers between devices, body(): lax.all_gather(up_weight, 'fsdp', axis=0, tiled=True)  125 us
    all_gather x1, waiting for transfers between devices, body(): lax.all_gather(down_weight, 'fsdp', axis=0, tiled=True)  124 us
    all_gather x1, waiting for transfers between devices, body(): lax.all_gather(gate_weight, 'fsdp', axis=0, tiled=True)  99.9 us
    all_to_all x1, waiting for transfers between devices, body(): lax.all_to_all(out_slots, 'fsdp', split_axis=1, concat_axis=0, tiled=True)  95.6 us
    all_to_all x1, blocking collectives, body(): lax.all_to_all(sent_tokens, 'fsdp', split_axis=0, concat_axis=1, tiled=True)  92.7 us
  transfers between devices with their start and end apart: 18, of which 11 were waited for; matrix products, arithmetic and copies ran while one was open for 12% of the time, Pallas kernels for 0%

profile of v1, /device:TPU:0, one launch (start us, length us, event | category | flops | bytes accessed | tf_op | source)
XLA Modules:
  0.0 1829.9 jit_solution(16258065482002926877)
XLA Ops:
  19.7 92.7 %all_to_all.71 = bf16[16,64,1024]{2,1,0:T(8,128)(2,1)} all-to-all(bf16[16,64,1024]{2,1,0:T(8,128)(2,1)S(1)} %get-tuple-element.59), channel_id=1, replica_groups=mesh['rep'=4,'fsdp'=8] {'fsdp'}, dimensions={0} | all-to-all | bytes 4194304 | tf_op jit(solution)/shard_map/all_to_all | solution.py:251
  119.0 68.1 %all-gather = bf16[8,1,128]{2,1,0:T(2,128)(2,1)S(1)} all-gather(bf16[1,1,128]{2,1,0:T(2,128)(2,1)S(1)} %bitcast.87), channel_id=1, replica_groups=mesh['rep'=4,'fsdp'=8] {'fsdp'}, dimensions={0}, use_global_device_ids=true | all-gather | bytes 2304 | tf_op jit(solution)/shard_map/all_gather | solution.py:257
  187.1 30.4 %all-gather.1 = bf16[8,1,128]{2,1,0:T(2,128)(2,1)S(1)} all-gather(bf16[1,1,128]{2,1,0:T(2,128)(2,1)S(1)} %bitcast.88), channel_id=1, replica_groups=mesh['rep'=4,'fsdp'=8] {'fsdp'}, dimensions={0}, use_global_device_ids=true | all-gather | bytes 2304 | tf_op jit(solution)/shard_map/all_gather | solution.py:263
  217.5 16.5 all_gather.33
  273.8 99.9 %all-gather.12.cloned.1.call-done = bf16[1024,4608]{1,0:T(8,128)(2,1)} async-done(((bf16[128,4608]{1,0:T(8,128)(2,1)}), bf16[1024,4608]{1,0:T(8,128)(2,1)}) %all-gather.12.cloned.1.call-update) | async-done | bytes 9437200 | tf_op jit(solution)/shard_map/all_gather | solution.py:264
  373.7 13.4 fusion.55
  387.1 125.0 %all-gather.14.cloned.1.call-done = bf16[1024,4608]{1,0:T(8,128)(2,1)} async-done(((bf16[128,4608]{1,0:T(8,128)(2,1)}), bf16[1024,4608]{1,0:T(8,128)(2,1)}) %all-gather.14.cloned.1.call-update) | async-done | bytes 9437200 | tf_op jit(solution)/shard_map/all_gather | solution.py:265
  512.1 13.9 fusion.56
  526.0 124.4 %all-gather.16.cloned.1.call-done = bf16[4608,1024]{1,0:T(8,128)(2,1)} async-done(((bf16[576,1024]{1,0:T(8,128)(2,1)}), bf16[4608,1024]{1,0:T(8,128)(2,1)}) %all-gather.16.cloned.1.call-update) | async-done | bytes 9437200 | tf_op jit(solution)/shard_map/all_gather | solution.py:284
  650.4 27.9 %multiply_convert_fusion = (bf16[768,4608]{1,0:T(8,128)(2,1)}, bf16[768,4608]{1,0:T(8,128)(2,1)}, bf16[768,4608]{1,0:T(8,128)(2,1)}) fusion(f32[768,4608]{1,0:T(8,128)} %fusion.55, f32[768,4608]{1,0:T(8,128)} %fusion.56, bf16[4608,1024]{1,0:T(8,128)(2,1)} %all-gather.16.cloned.1.call-done, pred[768]{0:T(1024)(128)(4,1)S(1)} %iota_compare_fusion.2, ...), kind=kOutput, calls=%fused_computation.8 | convolution fusion | flops 7307526144 | bytes 60556800 | tf_op jit(solution)/shard_map/dot_general | solution.py:48
  678.3 13.5 fusion.57
  737.6 13.0 convolution_convert_fusion.2
  750.7 12.9 convolution_convert_fusion.1
  765.4 13.7 convolution_convert_fusion
  779.1 19.3 %collective-permute-done = bf16[576,1024]{1,0:T(8,128)(2,1)} collective-permute-done((bf16[576,1024]{1,0:T(8,128)(2,1)S(1)}, bf16[576,1024]{1,0:T(8,128)(2,1)}, u32[]{:S(2)}, u32[]{:S(2)}) %collective-permute-start) | collective-permute-done | bytes 1179680 | tf_op jit(solution)/shard_map/ppermute | solution.py:15
  801.7 87.6 %collective-permute-done.1 = bf16[1152,1024]{1,0:T(8,128)(2,1)} collective-permute-done((bf16[1152,1024]{1,0:T(8,128)(2,1)}, bf16[1152,1024]{1,0:T(8,128)(2,1)}, u32[]{:S(2)}, u32[]{:S(2)}) %collective-permute-start.1) | collective-permute-done | bytes 2359328 | tf_op jit(solution)/shard_map/ppermute | solution.py:15
  898.1 304.9 %collective-permute-done.2 = bf16[2304,1024]{1,0:T(8,128)(2,1)} collective-permute-done((bf16[2304,1024]{1,0:T(8,128)(2,1)}, bf16[2304,1024]{1,0:T(8,128)(2,1)}, u32[]{:S(2)}, u32[]{:S(2)}) %collective-permute-start.2) | collective-permute-done | bytes 4718624 | tf_op jit(solution)/shard_map/ppermute | solution.py:15
  1203.0 14.1 fusion.28
  1255.6 95.6 %all-to-all-done.1 = bf16[2,512,1024]{2,0,1:T(2,128)(2,1)} async-done(((bf16[2,512,1024]{2,0,1:T(2,128)(2,1)}), bf16[2,512,1024]{2,0,1:T(2,128)(2,1)}, u32[]{:S(2)}, u32[]{:S(2)}) %all-to-all-start.1) | async-done | bytes 2097184 | tf_op jit(solution)/shard_map/all_to_all | solution.py:270
  1356.0 133.8 %reduce-scatter.15.cloned.1.call-done = bf16[128,4608]{1,0:T(8,128)(2,1)} async-done(((bf16[1024,4608]{1,0:T(8,128)(2,1)}), bf16[128,4608]{1,0:T(8,128)(2,1)}) %reduce-scatter.15.cloned.1.call-update) | async-done | bytes 1179664 | tf_op jit(solution)/shard_map/reduce_scatter | solution.py:310
  1489.8 166.0 %reduce-scatter.17.cloned.1.call-done = bf16[576,1024]{1,0:T(8,128)(2,1)} async-done(((bf16[4608,1024]{1,0:T(8,128)(2,1)}), bf16[576,1024]{1,0:T(8,128)(2,1)}) %reduce-scatter.17.cloned.1.call-update) | async-done | bytes 1179664 | tf_op jit(solution)/shard_map/reduce_scatter | solution.py:313
  1657.2 19.5 %all-reduce.6 = (bf16[1024]{0:T(1024)(128)(2,1)S(1)}, bf16[1024]{0:T(1024)(128)(2,1)S(1)}) all-reduce(bf16[1024]{0:T(1024)(128)(2,1)S(1)} %get-tuple-element.18, bf16[1024]{0:T(1024)(128)(2,1)S(1)} %get-tuple-element.13), channel_id=2, replica_groups=mesh['rep'=4,'fsdp'=8] {'fsdp'}, use_global_device_ids=true, to_apply=%region_11.15.clone | all-reduce | flops 2048 | bytes 8192
  1676.8 43.3 %reduce-scatter.19.cloned.1.call-done = bf16[128,3]{1,0:T(8,128)(2,1)} async-done(((bf16[1024,3]{1,0:T(8,128)(2,1)}), bf16[128,3]{1,0:T(8,128)(2,1)}) %reduce-scatter.19.cloned.1.call-update) | async-done | bytes 784
  1744.7 69.7 %all-reduce.11.cloned.1.call-done = (bf16[128,3072]{1,0:T(8,128)(2,1)}, bf16[128,1024]{1,0:T(8,128)(2,1)}, bf16[128,4608]{1,0:T(8,128)(2,1)}, bf16[128,4608]{1,0:T(8,128)(2,1)}, bf16[576,1024]{1,0:T(8,128)(2,1)}) async-done(((bf16[128,3072]{1,0:T(8,128)(2,1)}, bf16[128,1024]{1,0:T(8,128)(2,1)}, bf16[128,4608]{1,0:T(8,128)(2,1)}, bf16[128,4608]{1,0:T(8,128)(2,1)}, bf16[576,1024]{1,0:T(8,128)(2,1)}), ...) | async-done | bytes 4587536 | tf_op jit(solution)/shard_map/psum | solution.py:319
  (192 shorter events, 195.3 us)
Async XLA Ops:
  7.2 244.2 %all-gather.8.cloned.1.call-start = ((), (), s32[]{:S(2)}) async-start(), calls=%async_computation.10 | async-start | bytes 7077888 | tf_op jit(solution)/shard_map/all_gather | solution.py:258
  7.9 258.6 %all-gather.10.cloned.1.call-start = ((), (), s32[]{:S(2)}) async-start(), calls=%async_computation.11 | async-start | bytes 2359296 | tf_op jit(solution)/shard_map/all_gather | solution.py:260
  8.7 365.1 %all-gather.12.cloned.1.call-start = ((), (), s32[]{:S(2)}) async-start(), calls=%async_computation.12 | async-start | bytes 10616832 | tf_op jit(solution)/shard_map/all_gather | solution.py:264
  9.4 502.6 %all-gather.14.cloned.1.call-start = ((), (), s32[]{:S(2)}) async-start(), calls=%async_computation.13 | async-start | bytes 10616832 | tf_op jit(solution)/shard_map/all_gather | solution.py:265
  10.0 640.4 %all-gather.16.cloned.1.call-start = ((), (), s32[]{:S(2)}) async-start(), calls=%async_computation.14 | async-start | bytes 10616832 | tf_op jit(solution)/shard_map/all_gather | solution.py:284
  112.5 74.6 %copy-start.31 = (bf16[128]{0:T(256)(128)(2,1)S(1)}, bf16[128]{0:T(256)(128)(2,1)}, u32[]{:S(2)}) copy-start(bf16[128]{0:T(256)(128)(2,1)} %param.26) | copy-start | bytes 772
  112.5 105.1 %copy-start.29 = (bf16[128,3]{0,1:T(4,128)(2,1)S(1)}, bf16[128,3]{0,1:T(4,128)(2,1)}, u32[]{:S(2)}) copy-start(bf16[128,3]{0,1:T(4,128)(2,1)} %param.24) | copy-start | bytes 2308
  112.5 125.0 %all-to-all-start.2 = ((bf16[16,64,1024]{2,1,0:T(8,128)(2,1)}), bf16[16,64,1024]{2,1,0:T(8,128)(2,1)}, u32[]{:S(2)}, u32[]{:S(2)}) async-start(bf16[16,64,1024]{2,1,0:T(8,128)(2,1)} %get-tuple-element.58), calls=%async_computation.2 | async-start | bytes 4194304 | tf_op jit(solution)/shard_map/all_to_all | solution.py:252
  117.6 1238.3 %reduce-scatter.11.cloned.1.call-start = ((), (), s32[]{:S(2)}) async-start(), calls=%async_computation.16 | async-start | bytes 2359296 | tf_op jit(solution)/shard_map/reduce_scatter | solution.py:301
  709.5 646.5 %reduce-scatter.9.cloned.1.call-start = ((), (), s32[]{:S(2)}) async-start(), calls=%async_computation.15 | async-start | bytes 7077888 | tf_op jit(solution)/shard_map/reduce_scatter | solution.py:295
  736.2 619.8 %reduce-scatter.13.cloned.1.call-start = ((), (), s32[]{:S(2)}) async-start(), calls=%async_computation.17 | async-start | bytes 10616832 | tf_op jit(solution)/shard_map/reduce_scatter | solution.py:307
  750.7 739.1 %reduce-scatter.15.cloned.1.call-start = ((), (), s32[]{:S(2)}) async-start(), calls=%async_computation.18 | async-start | bytes 10616832 | tf_op jit(solution)/shard_map/reduce_scatter | solution.py:310
  763.7 892.1 %reduce-scatter.17.cloned.1.call-start = ((), (), s32[]{:S(2)}) async-start(), calls=%async_computation.19 | async-start | bytes 10616832 | tf_op jit(solution)/shard_map/reduce_scatter | solution.py:313
  764.9 33.5 %collective-permute-start = (bf16[576,1024]{1,0:T(8,128)(2,1)S(1)}, bf16[576,1024]{1,0:T(8,128)(2,1)}, u32[]{:S(2)}, u32[]{:S(2)}) collective-permute-start(bf16[576,1024]{1,0:T(8,128)(2,1)S(1)} %copy-done.15), channel_id=1, source_target_pairs={{0,1},{1,0},{2,3},{3,2},{4,5},{5,4},{6,7},{7,6},{8,9},{9,8},{10,11... | collective-permute-start | bytes 3538952 | tf_op jit(solution)/shard_map/ppermute | solution.py:15
  801.7 87.6 %collective-permute-start.1 = (bf16[1152,1024]{1,0:T(8,128)(2,1)}, bf16[1152,1024]{1,0:T(8,128)(2,1)}, u32[]{:S(2)}, u32[]{:S(2)}) collective-permute-start(bf16[1152,1024]{1,0:T(8,128)(2,1)} %maximum_select_fusion.3), channel_id=1, source_target_pairs={{0,2},{1,3},{2,0},{3,1},{4,6},{5,7},{6,4},{7,5},{8,10},{9,11},{10,... | collective-permute-start | bytes 7077896 | tf_op jit(solution)/shard_map/ppermute | solution.py:15
  801.7 96.3 %copy-start.26 = (s32[2]{0:T(128)S(1)}, s32[2]{0:T(128)}, u32[]{:S(2)}) copy-start(s32[2]{0:T(128)} %copy-done.25) | copy-start | bytes 28
  801.7 96.3 %copy-start.28 = (s32[2]{0:T(128)S(1)}, s32[2]{0:T(128)}, u32[]{:S(2)}) copy-start(s32[2]{0:T(128)} %get-tuple-element.60) | copy-start | bytes 28
  895.6 307.4 %collective-permute-start.2 = (bf16[2304,1024]{1,0:T(8,128)(2,1)}, bf16[2304,1024]{1,0:T(8,128)(2,1)}, u32[]{:S(2)}, u32[]{:S(2)}) collective-permute-start(bf16[2304,1024]{1,0:T(8,128)(2,1)} %maximum_select_fusion.2), channel_id=1, source_target_pairs={{0,4},{1,5},{2,6},{3,7},{4,0},{5,1},{6,2},{7,3},{8,12},{9,13},{10,... | collective-permute-start | bytes 14155784 | tf_op jit(solution)/shard_map/ppermute | solution.py:15
  1245.8 105.3 %all-to-all-start.1 = ((bf16[2,512,1024]{2,0,1:T(2,128)(2,1)}), bf16[2,512,1024]{2,0,1:T(2,128)(2,1)}, u32[]{:S(2)}, u32[]{:S(2)}) async-start(bf16[2,512,1024]{2,0,1:T(2,128)(2,1)} %copy.39), calls=%async_computation.1 | async-start | bytes 4194304 | tf_op jit(solution)/shard_map/all_to_all | solution.py:270
  1351.2 380.7 %all-to-all-start.3 = ((bf16[2,512,1024]{2,0,1:T(2,128)(2,1)}), bf16[2,512,1024]{2,0,1:T(2,128)(2,1)S(1)}, u32[]{:S(2)}, u32[]{:S(2)}) async-start(bf16[2,512,1024]{2,0,1:T(2,128)(2,1)} %copy.43), calls=%async_computation.3 | async-start | bytes 4194304 | tf_op jit(solution)/shard_map/all_to_all | solution.py:289
  1354.8 301.0 %copy-start.34 = (u32[32]{0:T(128)S(1)}, u32[32]{0:T(128)}, u32[]{:S(2)}) copy-start(u32[32]{0:T(128)} %constant.111) | copy-start | bytes 388
  1354.8 302.2 %copy-start.33 = (s32[1,16]{1,0:T(1,128)S(1)}, s32[1,16]{1,0:T(1,128)}, u32[]{:S(2)}) copy-start(s32[1,16]{1,0:T(1,128)} %param.21) | copy-start | bytes 196
  1354.8 365.3 %reduce-scatter.19.cloned.1.call-start = ((), (), s32[]{:S(2)}) async-start(), calls=%async_computation.20 | async-start | bytes 294912
  1355.8 458.5 %all-reduce.11.cloned.1.call-start = ((), (), s32[]{:S(2)}) async-start(), calls=%async_computation.21 | async-start | bytes 9175040 | tf_op jit(solution)/shard_map/psum | solution.py:319
  (30 other events, 141.9 us)
Sparse Core Ops, SparseCore 0:
  10.2 174.4 all-gather.7
  186.8 48.0 all-gather.9
  237.1 136.5 all-gather.11
  375.8 136.2 all-gather.13
  514.1 136.2 all-gather.15
  709.6 66.4 reduce-scatter.10
  779.7 259.5 reduce-scatter.8
  1042.8 201.0 reduce-scatter.12
  1247.5 242.1 reduce-scatter.14
  1493.2 162.5 reduce-scatter.16
  1659.7 60.3 reduce-scatter.18
  1722.7 91.6 all-reduce.10
